TPU v7x, 32 devices: a whole 2x2x4 slice. The times are simulated.
32 devices in a mesh: shard: 2 (over y), ctx: 4 (over x, core), tp: 4 (over z).
Axes of the slice: x: 2, y: 2, z: 4, core: 2. Of those that a mesh axis runs over, the one named last changes fastest.
Arguments:
- video: bfloat16 [2, 16, 16, 16, 1152], P('shard', 'ctx', 'tp'), may hold values from -6 to 6
- cond: bfloat16 [2, 1152], P('shard'), may hold values from -6 to 6
- w_ada: bfloat16 [2, 1152, 6912], P(None, 'shard', 'tp'), may hold values from -0.1875 to 0.1875
- b_ada: bfloat16 [2, 6912], P(None, 'tp'), may hold values from 0.5 to 1.5
- w_qkv: bfloat16 [2, 3, 1152, 1152], P(None, None, 'shard', 'tp'), may hold values from -0.09375 to 0.09375
- b_qv: bfloat16 [2, 2, 1152], P(None, None, 'tp'), may hold values from -3 to 3
- w_out: bfloat16 [2, 1152, 1152], P(None, 'tp', 'shard'), may hold values from -0.75 to 0.75
- b_out: bfloat16 [2, 1152], replicated, may hold values from -3 to 3
- w_up: bfloat16 [2, 1152, 4608], P(None, 'shard', 'tp'), may hold values from -0.09375 to 0.09375
- b_up: bfloat16 [2, 4608], P(None, 'tp'), may hold values from -3 to 3
- w_down: bfloat16 [2, 4608, 1152], P(None, 'tp', 'shard'), may hold values from -0.09375 to 0.09375
- b_down: bfloat16 [2, 1152], replicated, may hold values from -3 to 3
- cotangent: bfloat16 [2, 16, 16, 16, 1152], P('shard', None, 'tp', 'ctx'), may hold values from -6 to 6
Outputs:
- out: bfloat16 [2, 16, 16, 16, 1152], P('shard', None, 'tp', 'ctx')
- grad_video: float32 [2, 16, 16, 16, 1152], P('shard', 'ctx', 'tp')
- grad_cond: float32 [2, 1152], P('shard')
- grad_w_ada: float32 [2, 1152, 6912], P(None, 'shard', 'tp')
- grad_b_ada: float32 [2, 6912], P(None, 'tp')
- grad_w_qkv: float32 [2, 3, 1152, 1152], P(None, None, 'shard', 'tp')
- grad_b_qv: float32 [2, 2, 1152], P(None, None, 'tp')
- grad_w_out: float32 [2, 1152, 1152], P(None, 'tp', 'shard')
- grad_b_out: float32 [2, 1152], replicated
- grad_w_up: float32 [2, 1152, 4608], P(None, 'shard', 'tp')
- grad_b_up: float32 [2, 4608], P(None, 'tp')
- grad_w_down: float32 [2, 4608, 1152], P(None, 'tp', 'shard')
- grad_b_down: float32 [2, 1152], replicated
All inputs are finite; a program needn't handle non-finite values.
Results may differ from a plain program's by a relative error of at most 0.025.
Values may be sent and summed in bfloat16 or wider, within the bound.
No kernel may reach another device: no remote copies, remote signals or barrier semaphores. Data moves between devices by JAX's collectives and lax.ppermute only.
A program may use at most 256 MiB of HBM per device.

v0:
```python
from functools import partial
import math
import jax
import jax.numpy as jnp
from jax import lax
from jax.sharding import PartitionSpec as P

HEAD_DIM = 72
highest = lax.Precision.HIGHEST


def layer_norm(values):
    average = jnp.mean(values, axis=-1, keepdims=True)
    centered = values - average
    spread = jnp.mean(centered * centered, axis=-1, keepdims=True)
    return centered * lax.rsqrt(spread + 1e-06)


def modulate(values, offset, factor):
    return layer_norm(values) * (1.0 + factor) + offset


def split_mod(modulation):
    pieces = modulation.reshape(modulation.shape[0], 6, 1, 1, 1, modulation.shape[1] // 6)
    return [pieces[:, number] for number in range(6)]


def to_sequences(rows, grid, temporal):
    heads = rows.reshape(grid + (-1, HEAD_DIM))
    head_count = heads.shape[5]
    if temporal:
        heads = jnp.transpose(heads, (0, 1, 3, 4, 2, 5, 6))
        return heads.reshape(-1, grid[2], head_count, HEAD_DIM)
    heads = jnp.transpose(heads, (1, 2, 0, 3, 4, 5, 6))
    return heads.reshape(grid[1] * grid[2], -1, head_count, HEAD_DIM)


def from_sequences(heads, grid, temporal):
    head_count = heads.shape[2]
    if temporal:
        heads = heads.reshape(grid[0], grid[1], grid[3], grid[4], grid[2], head_count, HEAD_DIM)
        heads = jnp.transpose(heads, (0, 1, 4, 2, 3, 5, 6))
    else:
        heads = heads.reshape(grid[1], grid[2], grid[0], grid[3], grid[4], head_count, HEAD_DIM)
        heads = jnp.transpose(heads, (2, 0, 1, 3, 4, 5, 6))
    return heads.reshape(-1, head_count * HEAD_DIM)


def attend(query_seq, key_seq, value_seq):
    factor = 1.0 / math.sqrt(HEAD_DIM)
    scores = (
        jnp.einsum("bqhe,bkhe->bhqk", query_seq, key_seq, preferred_element_type=jnp.float32)
        * factor
    )
    row_max = jnp.max(scores, axis=-1, keepdims=True)
    weights = jnp.exp(scores - row_max)
    totals = jnp.sum(weights, axis=-1, keepdims=True)
    probs_low = (weights / totals).astype(jnp.bfloat16)
    attended = jnp.einsum(
        "bhqk,bkhe->bqhe", probs_low, value_seq, preferred_element_type=jnp.float32
    )
    return (attended.astype(jnp.bfloat16), row_max + jnp.log(totals))


def attend_back(query_seq, key_seq, value_seq, log_total, grad_out):
    factor = 1.0 / math.sqrt(HEAD_DIM)
    scores = (
        jnp.einsum("bqhe,bkhe->bhqk", query_seq, key_seq, preferred_element_type=jnp.float32)
        * factor
    )
    probs = jnp.exp(scores - log_total)
    grad_value = jnp.einsum(
        "bhqk,bqhe->bkhe", probs.astype(jnp.bfloat16), grad_out, preferred_element_type=jnp.float32
    ).astype(jnp.bfloat16)
    grad_probs = jnp.einsum(
        "bqhe,bkhe->bhqk", grad_out, value_seq, preferred_element_type=jnp.float32
    )
    inner = jnp.sum(grad_probs * probs, axis=-1, keepdims=True)
    grad_scores = (probs * (grad_probs - inner)).astype(jnp.bfloat16)
    grad_query = (
        jnp.einsum("bhqk,bkhe->bqhe", grad_scores, key_seq, preferred_element_type=jnp.float32)
        * factor
    ).astype(jnp.bfloat16)
    grad_key = (
        jnp.einsum("bhqk,bqhe->bkhe", grad_scores, query_seq, preferred_element_type=jnp.float32)
        * factor
    ).astype(jnp.bfloat16)
    return (grad_query, grad_key, grad_value)


def fetch_forward(number, w_ada, w_qkv, w_out, w_up, w_down):
    return (
        lax.all_gather(w_ada[number], "shard", axis=0, tiled=True),
        lax.all_gather(w_qkv[number], "shard", axis=1, tiled=True),
        lax.all_gather(w_out[number], "shard", axis=1, tiled=True),
        lax.all_gather(w_up[number], "shard", axis=0, tiled=True),
        lax.all_gather(w_down[number], "shard", axis=1, tiled=True),
    )


def fetch_again(number, w_ada, w_qkv, w_out, w_up, w_down):
    return (
        lax.all_gather(w_ada[number], "shard", axis=0, tiled=True),
        lax.all_gather(w_qkv[number], "shard", axis=1, tiled=True),
        lax.all_gather(w_out[number], "shard", axis=1, tiled=True),
        lax.all_gather(w_up[number], "shard", axis=0, tiled=True),
        lax.all_gather(w_down[number], "shard", axis=1, tiled=True),
    )


def spread_rows(values):
    return lax.all_gather(values[None], "tp", axis=0, tiled=True)


def spread_grads(values):
    return lax.all_gather(values[None], "tp", axis=0, tiled=True)


def reduce_rows(term, own_rows):
    return lax.psum_scatter(
        term(jnp.int32(0), own_rows * lax.axis_size("tp")), "tp", scatter_dimension=0, tiled=True
    )


def reduce_grads(term, own_rows):
    return lax.psum_scatter(
        term(jnp.int32(0), own_rows * lax.axis_size("tp")), "tp", scatter_dimension=0, tiled=True
    )


def sum_weight_grads(grads):
    summed = (
        lax.psum_scatter(
            grads[0].astype(jnp.bfloat16), "shard", scatter_dimension=0, tiled=True
        ).astype(jnp.float32),
        lax.psum_scatter(
            grads[1].astype(jnp.bfloat16), "shard", scatter_dimension=1, tiled=True
        ).astype(jnp.float32),
        lax.psum_scatter(
            grads[2].astype(jnp.bfloat16), "shard", scatter_dimension=1, tiled=True
        ).astype(jnp.float32),
        lax.psum_scatter(
            grads[3].astype(jnp.bfloat16), "shard", scatter_dimension=0, tiled=True
        ).astype(jnp.float32),
        lax.psum_scatter(
            grads[4].astype(jnp.bfloat16), "shard", scatter_dimension=1, tiled=True
        ).astype(jnp.float32),
    )
    return (
        lax.psum(summed[0].astype(jnp.bfloat16), "ctx").astype(jnp.float32),
        lax.psum(summed[1].astype(jnp.bfloat16), "ctx").astype(jnp.float32),
        lax.psum(summed[2].astype(jnp.bfloat16), "ctx").astype(jnp.float32),
        lax.psum(summed[3].astype(jnp.bfloat16), "ctx").astype(jnp.float32),
        lax.psum(summed[4].astype(jnp.bfloat16), "ctx").astype(jnp.float32),
    )


def row_product(left, right, first_row, row_count):
    return jnp.dot(left, right, preferred_element_type=jnp.float32)


def row_product_back(left, right, first_row, row_count):
    return jnp.einsum("rf,df->rd", left, right, preferred_element_type=jnp.float32)


def qkv_product_back(left, right, first_row, row_count):
    return jnp.einsum("trc,tdc->rd", left, right, preferred_element_type=jnp.float32)


def forward_block(inputs, cond_act, gathered, b_ada, b_qv, b_out, b_up, b_down, temporal):
    ada_full, qkv_full, out_full, up_full, down_full = gathered
    width = inputs.shape[-1]
    own_rows = inputs.shape[0] * inputs.shape[1] * inputs.shape[2] * inputs.shape[3]
    mod_part = jnp.dot(cond_act, ada_full, preferred_element_type=jnp.float32) + b_ada
    modulation = lax.all_gather(mod_part, "tp", axis=1, tiled=True)
    shift_a, scale_a, gate_a, shift_m, scale_m, gate_m = split_mod(modulation)
    hidden = spread_rows(modulate(inputs, shift_a, scale_a).astype(jnp.bfloat16))
    grid = hidden.shape[:5]
    hidden_rows = hidden.reshape(-1, width)
    projected = jnp.einsum("rd,tdc->trc", hidden_rows, qkv_full, preferred_element_type=jnp.float32)
    query_seq = to_sequences((projected[0] + b_qv[0]).astype(jnp.bfloat16), grid, temporal)
    key_seq = to_sequences(projected[1].astype(jnp.bfloat16), grid, temporal)
    value_seq = to_sequences((projected[2] + b_qv[1]).astype(jnp.bfloat16), grid, temporal)
    attended, log_total = attend(query_seq, key_seq, value_seq)
    attended_rows = from_sequences(attended, grid, temporal)
    attn_out = (
        reduce_rows(partial(row_product, attended_rows, out_full), own_rows) + b_out
    ).reshape(inputs.shape)
    after_attn = inputs + gate_a * attn_out
    hidden_two = spread_rows(modulate(after_attn, shift_m, scale_m).astype(jnp.bfloat16)).reshape(
        -1, width
    )
    up_rows = jnp.dot(hidden_two, up_full, preferred_element_type=jnp.float32) + b_up
    activated = jax.nn.gelu(up_rows, approximate=True).astype(jnp.bfloat16)
    mlp_out = (reduce_rows(partial(row_product, activated, down_full), own_rows) + b_down).reshape(
        inputs.shape
    )
    result = after_attn + gate_m * mlp_out
    kept = (
        inputs,
        after_attn,
        modulation,
        hidden_rows,
        query_seq,
        key_seq,
        value_seq,
        log_total,
        attended_rows,
        attn_out,
        hidden_two,
        up_rows,
        mlp_out,
        grid,
    )
    return (result, kept)


def backward_block(grad_y, kept, gathered, cond_act, temporal):
    (
        inputs,
        after_attn,
        modulation,
        hidden_rows,
        query_seq,
        key_seq,
        value_seq,
        log_total,
        attended_rows,
        attn_out,
        hidden_two,
        up_rows,
        mlp_out,
        grid,
    ) = kept
    ada_full, qkv_full, out_full, up_full, down_full = gathered
    width = inputs.shape[-1]
    clips = inputs.shape[0]
    own_rows = inputs.shape[0] * inputs.shape[1] * inputs.shape[2] * inputs.shape[3]
    shift_a, scale_a, gate_a, shift_m, scale_m, gate_m = split_mod(modulation)
    token_axes = (1, 2, 3)
    grad_mlp = (gate_m * grad_y).astype(jnp.bfloat16)
    grad_gate_m = jnp.sum(grad_y * mlp_out, axis=token_axes)
    grad_mlp_rows = spread_grads(grad_mlp).reshape(-1, width)
    grad_b_down = jnp.sum(grad_mlp_rows, axis=0, dtype=jnp.float32)
    activated, gelu_back = jax.vjp(partial(jax.nn.gelu, approximate=True), up_rows)
    grad_w_down = jnp.einsum(
        "rf,rd->fd",
        activated.astype(jnp.bfloat16),
        grad_mlp_rows,
        preferred_element_type=jnp.float32,
    )
    grad_act = jnp.einsum("rd,fd->rf", grad_mlp_rows, down_full, preferred_element_type=jnp.float32)
    grad_up = gelu_back(grad_act)[0].astype(jnp.bfloat16)
    grad_b_up = jnp.sum(grad_up, axis=0, dtype=jnp.float32)
    grad_w_up = jnp.einsum("rd,rf->df", hidden_two, grad_up, preferred_element_type=jnp.float32)
    grad_hidden_two = reduce_grads(partial(row_product_back, grad_up, up_full), own_rows).reshape(
        inputs.shape
    )
    unused_two, norm_back_two = jax.vjp(modulate, after_attn, shift_m, scale_m)
    grad_norm_two, grad_shift_m, grad_scale_m = norm_back_two(grad_hidden_two)
    grad_after = grad_y + grad_norm_two
    grad_attn = (gate_a * grad_after).astype(jnp.bfloat16)
    grad_gate_a = jnp.sum(grad_after * attn_out, axis=token_axes)
    grad_attn_rows = spread_grads(grad_attn).reshape(-1, width)
    grad_b_out = jnp.sum(grad_attn_rows, axis=0, dtype=jnp.float32)
    grad_w_out = jnp.einsum(
        "rc,rd->cd", attended_rows, grad_attn_rows, preferred_element_type=jnp.float32
    )
    grad_attended = jnp.einsum(
        "rd,cd->rc", grad_attn_rows, out_full, preferred_element_type=jnp.float32
    ).astype(jnp.bfloat16)
    grad_query, grad_key, grad_value = attend_back(
        query_seq, key_seq, value_seq, log_total, to_sequences(grad_attended, grid, temporal)
    )
    grad_proj = jnp.stack(
        [
            from_sequences(grad_query, grid, temporal),
            from_sequences(grad_key, grid, temporal),
            from_sequences(grad_value, grid, temporal),
        ]
    )
    grad_b_qv = jnp.stack(
        [
            jnp.sum(grad_proj[0], axis=0, dtype=jnp.float32),
            jnp.sum(grad_proj[2], axis=0, dtype=jnp.float32),
        ]
    )
    grad_w_qkv = jnp.einsum(
        "rd,trc->tdc", hidden_rows, grad_proj, preferred_element_type=jnp.float32
    )
    grad_hidden = reduce_grads(partial(qkv_product_back, grad_proj, qkv_full), own_rows).reshape(
        inputs.shape
    )
    unused_one, norm_back_one = jax.vjp(modulate, inputs, shift_a, scale_a)
    grad_norm_one, grad_shift_a, grad_scale_a = norm_back_one(grad_hidden)
    grad_inputs = grad_after + grad_norm_one
    grad_mod = jnp.concatenate(
        [
            grad_shift_a.reshape(clips, width),
            grad_scale_a.reshape(clips, width),
            grad_gate_a,
            grad_shift_m.reshape(clips, width),
            grad_scale_m.reshape(clips, width),
            grad_gate_m,
        ],
        axis=1,
    )
    grad_mod_part = lax.psum_scatter(grad_mod, "tp", scatter_dimension=1, tiled=True)
    grad_w_ada = jnp.dot(cond_act.astype(jnp.float32).T, grad_mod_part, precision=highest)
    grad_b_ada = jnp.sum(grad_mod_part, axis=0)
    grad_cond_part = jnp.dot(grad_mod_part, ada_full.astype(jnp.float32).T, precision=highest)
    summed = sum_weight_grads((grad_w_ada, grad_w_qkv, grad_w_out, grad_w_up, grad_w_down))
    biases = (grad_b_ada, grad_b_qv, grad_b_out, grad_b_up, grad_b_down)
    return (grad_inputs, summed, biases, grad_cond_part)


def body(
    video, cond, w_ada, b_ada, w_qkv, b_qv, w_out, b_out, w_up, b_up, w_down, b_down, cotangent
):
    cond_float = cond.astype(jnp.float32)
    silu_value, silu_back = jax.vjp(jax.nn.silu, cond_float)
    cond_act = silu_value.astype(jnp.bfloat16)
    first = fetch_forward(0, w_ada, w_qkv, w_out, w_up, w_down)
    middle, kept_one = forward_block(
        video.astype(jnp.float32),
        cond_act,
        first,
        b_ada[0],
        b_qv[0],
        b_out[0],
        b_up[0],
        b_down[0],
        False,
    )
    moved = lax.all_to_all(
        middle.astype(jnp.bfloat16), "ctx", split_axis=3, concat_axis=1, tiled=True
    )
    second = fetch_forward(1, w_ada, w_qkv, w_out, w_up, w_down)
    result, kept_two = forward_block(
        moved.astype(jnp.float32),
        cond_act,
        second,
        b_ada[1],
        b_qv[1],
        b_out[1],
        b_up[1],
        b_down[1],
        True,
    )
    second_back = fetch_again(1, w_ada, w_qkv, w_out, w_up, w_down)
    grad_moved, grads_two, biases_two, cond_two = backward_block(
        cotangent.astype(jnp.float32), kept_two, second_back, cond_act, True
    )
    grad_middle = lax.all_to_all(
        grad_moved.astype(jnp.bfloat16), "ctx", split_axis=1, concat_axis=3, tiled=True
    ).astype(jnp.float32)
    first_back = fetch_again(0, w_ada, w_qkv, w_out, w_up, w_down)
    grad_video, grads_one, biases_one, cond_one = backward_block(
        grad_middle, kept_one, first_back, cond_act, False
    )
    bias_sums = lax.psum(
        (
            jnp.stack([biases_one[0], biases_two[0]]),
            jnp.stack([biases_one[1], biases_two[1]]),
            jnp.stack([biases_one[2], biases_two[2]]),
            jnp.stack([biases_one[3], biases_two[3]]),
            jnp.stack([biases_one[4], biases_two[4]]),
        ),
        ("shard", "ctx"),
    )
    grad_act_total = lax.psum(cond_one + cond_two, ("ctx", "tp"))
    grad_cond = silu_back(grad_act_total)[0]
    return (
        result.astype(jnp.bfloat16),
        grad_video,
        grad_cond,
        jnp.stack([grads_one[0], grads_two[0]]),
        bias_sums[0],
        jnp.stack([grads_one[1], grads_two[1]]),
        bias_sums[1],
        jnp.stack([grads_one[2], grads_two[2]]),
        bias_sums[2],
        jnp.stack([grads_one[3], grads_two[3]]),
        bias_sums[3],
        jnp.stack([grads_one[4], grads_two[4]]),
        bias_sums[4],
    )


def solution(mesh):
    in_specs = (
        P("shard", "ctx", "tp", None, None),
        P("shard", None),
        P(None, "shard", "tp"),
        P(None, "tp"),
        P(None, None, "shard", "tp"),
        P(None, None, "tp"),
        P(None, "tp", "shard"),
        P(),
        P(None, "shard", "tp"),
        P(None, "tp"),
        P(None, "tp", "shard"),
        P(),
        P("shard", None, "tp", "ctx", None),
    )
    out_specs = (
        P("shard", None, "tp", "ctx", None),
        P("shard", "ctx", "tp", None, None),
        P("shard", None),
        P(None, "shard", "tp"),
        P(None, "tp"),
        P(None, None, "shard", "tp"),
        P(None, None, "tp"),
        P(None, "tp", "shard"),
        P(),
        P(None, "shard", "tp"),
        P(None, "tp"),
        P(None, "tp", "shard"),
        P(),
    )
    return jax.shard_map(body, mesh=mesh, in_specs=in_specs, out_specs=out_specs, check_vma=False)
```

profile of v0, /device:TPU:0, one launch (start us, length us, event | category | flops | bytes accessed | tf_op | source)
XLA Modules:
  0.0 2567.8 jit_solution(18138175500458335088)
XLA Ops:
  20.1 50.5 %all-gather.40.cloned.1.call-done = bf16[1,1152,1728]{2,1,0:T(8,128)(2,1)} async-done(((bf16[1,576,1728]{2,1,0:T(8,128)(2,1)}), bf16[1,1152,1728]{2,1,0:T(8,128)(2,1)}) %all-gather.40.cloned.1.call-update) | async-done | bytes 3981328 | tf_op jit(solution)/shard_map/all_gather | solution.py:93
  73.6 55.1 %all-gather.52.cloned.1.call-done = bf16[1,1152,1728]{2,1,0:T(8,128)(2,1)} async-done(((bf16[1,576,1728]{2,1,0:T(8,128)(2,1)}), bf16[1,1152,1728]{2,1,0:T(8,128)(2,1)}) %all-gather.52.cloned.1.call-update) | async-done | bytes 3981328 | tf_op jit(solution)/shard_map/all_gather | solution.py:93
  131.7 20.4 all-reduce.3
  156.8 40.7 %all-gather.4 = bf16[1,288,1152]{1,0,2:T(2,128)(2,1)S(1)} all-gather(bf16[1,288,576]{1,0,2:T(2,128)(2,1)S(1)} %copy.342), channel_id=6, replica_groups=mesh['shard'=2,'ctx'=4,'tp'=4] {'shard'}, dimensions={2}, use_global_device_ids=true | all-gather | bytes 995328 | tf_op jit(solution)/shard_map/all_gather | solution.py:95
  201.2 7.1 copy.225
  208.3 42.8 %all-gather.42.cloned.1.call-done = bf16[4,4,4,16,1152]{4,3,2,1,0:T(8,128)(2,1)} async-done(((bf16[1,4,4,16,1152]{4,3,2,1,0:T(8,128)(2,1)}), bf16[4,4,4,16,1152]{4,3,2,1,0:T(8,128)(2,1)}) %all-gather.42.cloned.1.call-update) | async-done | bytes 2359312 | tf_op jit(solution)/shard_map/all_gather | solution.py:112
  289.5 80.0 %reduce-scatter.33.cloned.1.call-done = f32[256,1152]{1,0:T(8,128)} async-done(((f32[1024,1152]{1,0:T(8,128)}), f32[256,1152]{1,0:T(8,128)}) %reduce-scatter.33.cloned.1.call-update) | async-done | bytes 1179664 | tf_op jit(solution)/shard_map/reduce_scatter | solution.py:120
  377.5 34.0 %all-gather.48.cloned.1.call-done = bf16[1,1152,1152]{2,1,0:T(8,128)(2,1)} async-done(((bf16[1,576,1152]{2,1,0:T(8,128)(2,1)}), bf16[1,1152,1152]{2,1,0:T(8,128)(2,1)}) %all-gather.48.cloned.1.call-update) | async-done | bytes 2654224 | tf_op jit(solution)/shard_map/all_gather | solution.py:96
  411.5 52.2 %all-gather.46.cloned.1.call-done = bf16[4,4,4,16,1152]{4,3,2,1,0:T(8,128)(2,1)} async-done(((bf16[1,4,4,16,1152]{4,3,2,1,0:T(8,128)(2,1)}), bf16[4,4,4,16,1152]{4,3,2,1,0:T(8,128)(2,1)}) %all-gather.46.cloned.1.call-update) | async-done | bytes 2359312 | tf_op jit(solution)/shard_map/all_gather | solution.py:112
  463.6 8.1 convolution_add_fusion.1
  471.8 32.1 %all-gather.50.cloned.1.call-done = bf16[1,1152,1152]{1,2,0:T(8,128)(2,1)} async-done(((bf16[1,1152,576]{1,2,0:T(8,128)(2,1)}), bf16[1,1152,1152]{1,2,0:T(8,128)(2,1)}) %all-gather.50.cloned.1.call-update) | async-done | bytes 2654224 | tf_op jit(solution)/shard_map/all_gather | solution.py:97
  503.9 9.6 fusion.37
  518.3 80.6 %reduce-scatter.35.cloned.1.call-done = f32[256,1152]{1,0:T(8,128)} async-done(((f32[1024,1152]{1,0:T(8,128)}), f32[256,1152]{1,0:T(8,128)}) %reduce-scatter.35.cloned.1.call-update) | async-done | bytes 1179664 | tf_op jit(solution)/shard_map/reduce_scatter | solution.py:120
  606.1 8.3 all-to-all-done
  628.0 41.5 %all-gather.11 = bf16[1,288,1152]{1,0,2:T(2,128)(2,1)S(1)} all-gather(bf16[1,288,576]{1,0,2:T(2,128)(2,1)} %copy.344), channel_id=13, replica_groups=mesh['shard'=2,'ctx'=4,'tp'=4] {'shard'}, dimensions={2}, use_global_device_ids=true | all-gather | bytes 995328 | tf_op jit(solution)/shard_map/all_gather | solution.py:95
  673.2 7.1 copy.248
  680.3 41.6 %all-gather.34.cloned.1.call-done = bf16[4,1,16,4,4,1152]{5,2,4,3,1,0:T(8,128)(2,1)} async-done(((bf16[1,1,16,4,4,1152]{5,2,4,3,1,0:T(8,128)(2,1)}), bf16[4,1,16,4,4,1152]{5,2,4,3,1,0:T(8,128)(2,1)}) %all-gather.34.cloned.1.call-update) | async-done | bytes 2359312 | tf_op jit(solution)/shard_map/all_gather | solution.py:112
  763.2 84.2 %reduce-scatter.37.cloned.1.call-done = f32[256,1152]{1,0:T(8,128)} async-done(((f32[1024,1152]{1,0:T(8,128)}), f32[256,1152]{1,0:T(8,128)}) %reduce-scatter.37.cloned.1.call-update) | async-done | bytes 1179664 | tf_op jit(solution)/shard_map/reduce_scatter | solution.py:120
  866.7 47.4 %all-gather.36.cloned.1.call-done = bf16[4,1,16,4,4,1152]{5,2,4,3,1,0:T(8,128)(2,1)} async-done(((bf16[1,1,16,4,4,1152]{5,2,4,3,1,0:T(8,128)(2,1)}), bf16[4,1,16,4,4,1152]{5,2,4,3,1,0:T(8,128)(2,1)}) %all-gather.36.cloned.1.call-update) | async-done | bytes 2359312 | tf_op jit(solution)/shard_map/all_gather | solution.py:112
  923.6 30.1 %all-gather.56.cloned.1.call-done = bf16[1,1152,1152]{2,1,0:T(8,128)(2,1)} async-done(((bf16[1,576,1152]{2,1,0:T(8,128)(2,1)}), bf16[1,1152,1152]{2,1,0:T(8,128)(2,1)}) %all-gather.56.cloned.1.call-update) | async-done | bytes 2654224 | tf_op jit(solution)/shard_map/all_gather | solution.py:96
  953.7 8.1 convolution_add_fusion
  961.8 32.6 %all-gather.58.cloned.1.call-done = bf16[1,1152,1152]{1,2,0:T(8,128)(2,1)} async-done(((bf16[1,1152,576]{1,2,0:T(8,128)(2,1)}), bf16[1,1152,1152]{1,2,0:T(8,128)(2,1)}) %all-gather.58.cloned.1.call-update) | async-done | bytes 2654224 | tf_op jit(solution)/shard_map/all_gather | solution.py:97
  994.5 9.5 fusion.28
  1004.0 42.4 %all-gather.60.cloned.1.call-done = bf16[4,16,4,4,1152]{4,1,3,2,0:T(8,128)(2,1)} async-done(((bf16[1,16,4,4,1152]{4,1,3,2,0:T(8,128)(2,1)}), bf16[4,16,4,4,1152]{4,1,3,2,0:T(8,128)(2,1)}) %all-gather.60.cloned.1.call-update) | async-done | bytes 2359312 | tf_op jit(solution)/shard_map/all_gather | solution.py:116
  1055.4 9.1 convert_reduce_fusion.4
  1079.1 53.6 %reduce-scatter.39.cloned.1.call-done = f32[256,1152]{1,0:T(8,128)} async-done(((f32[1024,1152]{1,0:T(8,128)}), f32[256,1152]{1,0:T(8,128)}) %reduce-scatter.39.cloned.1.call-update) | async-done | bytes 1179664 | tf_op jit(solution)/shard_map/reduce_scatter | solution.py:120
  1137.6 83.6 %reduce-scatter.41.cloned.1.call-done = f32[256,1152]{1,0:T(8,128)} async-done(((f32[1024,1152]{1,0:T(8,128)}), f32[256,1152]{1,0:T(8,128)}) %reduce-scatter.41.cloned.1.call-update) | async-done | bytes 1179664 | tf_op jit(solution)/shard_map/reduce_scatter | solution.py:126
  1241.0 49.7 %all-gather.62.cloned.1.call-done = bf16[4,16,4,4,1152]{4,1,3,2,0:T(8,128)(2,1)} async-done(((bf16[1,16,4,4,1152]{4,1,3,2,0:T(8,128)(2,1)}), bf16[4,16,4,4,1152]{4,1,3,2,0:T(8,128)(2,1)}) %all-gather.62.cloned.1.call-update) | async-done | bytes 2359312 | tf_op jit(solution)/shard_map/all_gather | solution.py:116
  1329.3 7.2 convolution_bitcast_fusion.1
  1338.0 82.7 %reduce-scatter.43.cloned.1.call-done = f32[256,1152]{1,0:T(8,128)} async-done(((f32[1024,1152]{1,0:T(8,128)}), f32[256,1152]{1,0:T(8,128)}) %reduce-scatter.43.cloned.1.call-update) | async-done | bytes 1179664 | tf_op jit(solution)/shard_map/reduce_scatter | solution.py:126
  1439.7 12.1 all_to_all.8
  1453.4 49.7 %all-gather.38.cloned.1.call-done = bf16[4,1,4,4,16,1152]{5,4,3,2,1,0:T(8,128)(2,1)} async-done(((bf16[1,1,4,4,16,1152]{5,4,3,2,1,0:T(8,128)(2,1)}), bf16[4,1,4,4,16,1152]{5,4,3,2,1,0:T(8,128)(2,1)}) %all-gather.38.cloned.1.call-update) | async-done | bytes 2359312 | tf_op jit(solution)/shard_map/all_gather | solution.py:116
  1503.1 9.6 convert_reduce_fusion.5
  1520.9 82.7 %reduce-scatter.45.cloned.1.call-done = f32[256,1152]{1,0:T(8,128)} async-done(((f32[1024,1152]{1,0:T(8,128)}), f32[256,1152]{1,0:T(8,128)}) %reduce-scatter.45.cloned.1.call-update) | async-done | bytes 1179664 | tf_op jit(solution)/shard_map/reduce_scatter | solution.py:126
  1611.2 50.6 %all-gather.64.cloned.1.call-done = bf16[4,4,4,16,1152]{4,3,2,1,0:T(8,128)(2,1)} async-done(((bf16[1,4,4,16,1152]{4,3,2,1,0:T(8,128)(2,1)}), bf16[4,4,4,16,1152]{4,3,2,1,0:T(8,128)(2,1)}) %all-gather.64.cloned.1.call-update) | async-done | bytes 2359312 | tf_op jit(solution)/shard_map/all_gather | solution.py:116
  1705.3 7.2 convolution_bitcast_fusion
  1719.6 77.2 %reduce-scatter.47.cloned.1.call-done = f32[256,1152]{1,0:T(8,128)} async-done(((f32[1024,1152]{1,0:T(8,128)}), f32[256,1152]{1,0:T(8,128)}) %reduce-scatter.47.cloned.1.call-update) | async-done | bytes 1179664 | tf_op jit(solution)/shard_map/reduce_scatter | solution.py:126
  1807.4 5.8 fusion.24
  1813.2 7.2 copy.333
  1820.4 7.5 reshape.1236
  1833.0 5.8 fusion.23
  1838.8 7.2 copy.331
  1846.0 7.4 reshape.1234
  1853.5 7.1 convolution_convert_fusion.2
  1860.7 8.0 convolution_convert_fusion
  1869.0 8.0 convolution_convert_fusion.1
  1877.0 7.1 convolution_convert_fusion.3
  1886.4 49.3 %reduce-scatter.61.cloned.1.call-done = f32[1728,1]{1,0:T(8,128)} async-done(((f32[6912,1]{1,0:T(8,128)}), f32[1728,1]{1,0:T(8,128)}) %reduce-scatter.61.cloned.1.call-update) | async-done | bytes 6928 | tf_op jit(solution)/shard_map/reshape.135
  1937.1 6.1 multiply_convert_fusion.1
  1943.8 13.3 reduce-scatter.71.cloned.1.call-done
  1959.0 31.9 %reduce-scatter.67.cloned.1.call-done = bf16[576,864]{1,0:T(8,128)(2,1)} async-done(((bf16[1152,864]{1,0:T(8,128)(2,1)}), bf16[576,864]{1,0:T(8,128)(2,1)}) %reduce-scatter.67.cloned.1.call-update) | async-done | bytes 995344
  1997.7 14.2 reduce-scatter.69.cloned.1.call-done
  2013.8 31.7 %reduce-scatter.65.cloned.1.call-done = bf16[576,864]{1,0:T(8,128)(2,1)} async-done(((bf16[1152,864]{1,0:T(8,128)(2,1)}), bf16[576,864]{1,0:T(8,128)(2,1)}) %reduce-scatter.65.cloned.1.call-update) | async-done | bytes 995344
  2052.5 33.9 %reduce-scatter.55.cloned.1.call-done = bf16[576,1152]{1,0:T(8,128)(2,1)} async-done(((bf16[1152,1152]{1,0:T(8,128)(2,1)}), bf16[576,1152]{1,0:T(8,128)(2,1)}) %reduce-scatter.55.cloned.1.call-update) | async-done | bytes 1327120 | tf_op jit(solution)/shard_map/reduce_scatter | solution.py:142
  2086.4 40.3 %reduce-scatter.59.cloned.1.call-done = bf16[1152,576]{0,1:T(8,128)(2,1)} async-done(((bf16[1152,1152]{0,1:T(8,128)(2,1)}), bf16[1152,576]{0,1:T(8,128)(2,1)}) %reduce-scatter.59.cloned.1.call-update) | async-done | bytes 1327120 | tf_op jit(solution)/shard_map/reduce_scatter | solution.py:145
  2126.7 40.2 %reduce-scatter.57.cloned.1.call-done = bf16[1152,576]{0,1:T(8,128)(2,1)} async-done(((bf16[1152,1152]{0,1:T(8,128)(2,1)}), bf16[1152,576]{0,1:T(8,128)(2,1)}) %reduce-scatter.57.cloned.1.call-update) | async-done | bytes 1327120 | tf_op jit(solution)/shard_map/reduce_scatter | solution.py:145
  2166.9 40.9 %reduce-scatter.53.cloned.1.call-done = bf16[576,1152]{1,0:T(8,128)(2,1)} async-done(((bf16[1152,1152]{1,0:T(8,128)(2,1)}), bf16[576,1152]{1,0:T(8,128)(2,1)}) %reduce-scatter.53.cloned.1.call-update) | async-done | bytes 1327120 | tf_op jit(solution)/shard_map/reduce_scatter | solution.py:142
  2207.8 56.6 %reduce-scatter.49.cloned.1.call-done = bf16[576,1728]{1,0:T(8,128)(2,1)} async-done(((bf16[1152,1728]{1,0:T(8,128)(2,1)}), bf16[576,1728]{1,0:T(8,128)(2,1)}) %reduce-scatter.49.cloned.1.call-update) | async-done | bytes 1990672 | tf_op jit(solution)/shard_map/reduce_scatter | solution.py:133
  2264.4 56.4 %reduce-scatter.51.cloned.1.call-done = bf16[576,1728]{1,0:T(8,128)(2,1)} async-done(((bf16[1152,1728]{1,0:T(8,128)(2,1)}), bf16[576,1728]{1,0:T(8,128)(2,1)}) %reduce-scatter.51.cloned.1.call-update) | async-done | bytes 1990672 | tf_op jit(solution)/shard_map/reduce_scatter | solution.py:133
  2328.5 6.9 fusion.111
  2342.4 6.1 fusion.108
  2348.5 33.9 %psum.112 = f32[1,1152]{1,0:T(1,128)S(1)} all-reduce(f32[1,1152]{1,0:T(1,128)S(1)} %add.587), channel_id=1, replica_groups=mesh['shard'=2,'ctx'=4,'tp'=4] {'ctx','tp'}, use_global_device_ids=true, to_apply=%region_44.45 | all-reduce | flops 1152 | bytes 9216 | tf_op jit(solution)/shard_map/psum | solution.py:371
  2382.4 25.9 %all-reduce.2 = (f32[2,1728]{1,0:T(2,128)}, f32[2,2,288]{2,1,0:T(2,128)}, f32[2,1152]{1,0:T(2,128)}, f32[2,1152]{1,0:T(2,128)}, f32[2,1152]{1,0:T(2,128)}) all-reduce(f32[2,1728]{1,0:T(2,128)S(1)} %pad_maximum_fusion.6, f32[2,2,288]{2,1,0:T(2,128)S(1)} %pad_maximum_fusion.10, ...), channel_id=1, replica_groups=mesh['shard'=2,'ctx'=4,'tp'=4] {'shard','ctx'}, use_global_device_ids=true, to_apply=%region_49.50 | all-reduce | flops 11520 | bytes 92160 | tf_op jit(solution)/shard_map/psum | solution.py:361
  2408.9 135.4 %all-reduce.7.cloned.1.call-done = (bf16[1,576,1728]{2,1,0:T(8,128)(2,1)}, bf16[1,576,1728]{2,1,0:T(8,128)(2,1)}, bf16[1,3,576,288]{2,3,1,0:T(8,128)(2,1)}, bf16...) async-done(((bf16[1,576,1728]{2,1,0:T(8,128)(2,1)}, ...) | async-done | bytes 11943952 | tf_op jit(solution)/shard_map/psum | solution.py:150
  (628 shorter events, 415.4 us)
Async XLA Ops:
  7.2 63.4 %all-gather.40.cloned.1.call-start = ((), (), s32[]{:S(2)}) async-start(), calls=%async_computation.39 | async-start | bytes 6193152 | tf_op jit(solution)/shard_map/all_gather | solution.py:93
  11.7 117.0 %all-gather.52.cloned.1.call-start = ((), (), s32[]{:S(2)}) async-start(), calls=%async_computation.45 | async-start | bytes 6193152 | tf_op jit(solution)/shard_map/all_gather | solution.py:93
  12.5 188.8 %all-gather.44.cloned.1.call-start = ((), (), s32[]{:S(2)}) async-start(), calls=%async_computation.41 | async-start | bytes 5308416 | tf_op jit(solution)/shard_map/all_gather | solution.py:94
  17.4 233.7 %all-gather.42.cloned.1.call-start = ((), (), s32[]{:S(2)}) async-start(), calls=%async_computation.40 | async-start | bytes 2949120 | tf_op jit(solution)/shard_map/all_gather | solution.py:112
  17.7 135.0 %copy-start.62 = (f32[4,4,16]{2,1,0:T(4,128)}, f32[4,4,16]{2,1,0:T(4,128)S(1)}, u32[]{:S(2)}) copy-start(f32[4,4,16]{2,1,0:T(4,128)S(1)} %broadcast_multiply_fusion.3) | copy-start | bytes 3076
  18.1 55.3 %copy-start.96 = (f32[4,4,16]{2,1,0:T(4,128)}, f32[4,4,16]{2,1,0:T(4,128)S(1)}, u32[]{:S(2)}) copy-start(f32[4,4,16]{2,1,0:T(4,128)S(1)} %fusion.84) | copy-start | bytes 3076
  18.7 110.0 %copy-start.94 = (f32[1,1152]{1,0:T(1,128)}, f32[1,1152]{1,0:T(1,128)S(1)}, u32[]{:S(2)}) copy-start(f32[1,1152]{1,0:T(1,128)S(1)} %get-tuple-element.91) | copy-start | bytes 13828
  20.0 132.7 %copy-start.74 = (f32[4,4,16]{2,1,0:T(4,128)}, f32[4,4,16]{2,1,0:T(4,128)S(1)}, u32[]{:S(2)}) copy-start(f32[4,4,16]{2,1,0:T(4,128)S(1)} %fusion.129) | copy-start | bytes 3076
  73.5 80.4 %copy-start.124 = (bf16[2,2,288]{2,1,0:T(2,128)(2,1)S(1)}, bf16[2,2,288]{2,1,0:T(2,128)(2,1)}, u32[]{:S(2)}) copy-start(bf16[2,2,288]{2,1,0:T(2,128)(2,1)} %param.18) | copy-start | bytes 6916
  73.5 81.1 %copy-start.56 = (bf16[2,288,576]{2,1,0:T(8,128)(2,1)S(1)}, bf16[2,288,576]{2,1,0:T(8,128)(2,1)}, u32[]{:S(2)}) copy-start(bf16[2,288,576]{2,1,0:T(8,128)(2,1)} %param.19) | copy-start | bytes 1990660
  152.7 218.2 %copy-start.79 = (f32[1152]{0:T(1024)}, f32[1152]{0:T(1024)S(1)}, u32[]{:S(2)}) copy-start(f32[1152]{0:T(1024)S(1)} %get-tuple-element.60) | copy-start | bytes 13828
  152.7 219.4 %copy-start.69 = (f32[1152]{0:T(1024)}, f32[1152]{0:T(1024)S(1)}, u32[]{:S(2)}) copy-start(f32[1152]{0:T(1024)S(1)} %get-tuple-element.57) | copy-start | bytes 13828
  153.8 215.7 %reduce-scatter.33.cloned.1.call-start = ((), (), s32[]{:S(2)}) async-start(), calls=%async_computation.22 | async-start | bytes 5898240 | tf_op jit(solution)/shard_map/reduce_scatter | solution.py:120
  258.8 16.0 copy-start.22
  285.4 126.1 %all-gather.48.cloned.1.call-start = ((), (), s32[]{:S(2)}) async-start(), calls=%async_computation.43 | async-start | bytes 3981312 | tf_op jit(solution)/shard_map/all_gather | solution.py:96
  288.9 174.8 %all-gather.46.cloned.1.call-start = ((), (), s32[]{:S(2)}) async-start(), calls=%async_computation.42 | async-start | bytes 2949120 | tf_op jit(solution)/shard_map/all_gather | solution.py:112
  289.5 81.4 %copy-start.85 = (f32[1152]{0:T(1024)}, f32[1152]{0:T(1024)S(1)}, u32[]{:S(2)}) copy-start(f32[1152]{0:T(1024)S(1)} %get-tuple-element.68) | copy-start | bytes 13828
  373.2 130.7 %all-gather.50.cloned.1.call-start = ((), (), s32[]{:S(2)}) async-start(), calls=%async_computation.44 | async-start | bytes 3981312 | tf_op jit(solution)/shard_map/all_gather | solution.py:97
  376.8 222.1 %reduce-scatter.35.cloned.1.call-start = ((), (), s32[]{:S(2)}) async-start(), calls=%async_computation.23 | async-start | bytes 5898240 | tf_op jit(solution)/shard_map/reduce_scatter | solution.py:120
  513.5 159.7 %all-gather.54.cloned.1.call-start = ((), (), s32[]{:S(2)}) async-start(), calls=%async_computation.46 | async-start | bytes 5308416 | tf_op jit(solution)/shard_map/all_gather | solution.py:94
  517.6 82.7 %copy-start.81 = (f32[1152]{0:T(1024)S(1)}, f32[1152]{0:T(1024)}, u32[]{:S(2)}) copy-start(f32[1152]{0:T(1024)} %get-tuple-element.55) | copy-start | bytes 13828
  518.3 82.2 %copy-start.83 = (f32[1152]{0:T(1024)}, f32[1152]{0:T(1024)S(1)}, u32[]{:S(2)}) copy-start(f32[1152]{0:T(1024)S(1)} %get-tuple-element.64) | copy-start | bytes 13828
  601.5 13.0 all-to-all-start
  605.0 116.9 %all-gather.34.cloned.1.call-start = ((), (), s32[]{:S(2)}) async-start(), calls=%async_computation.24 | async-start | bytes 2949120 | tf_op jit(solution)/shard_map/all_gather | solution.py:112
  624.7 222.7 %reduce-scatter.37.cloned.1.call-start = ((), (), s32[]{:S(2)}) async-start(), calls=%async_computation.25 | async-start | bytes 5898240 | tf_op jit(solution)/shard_map/reduce_scatter | solution.py:120
  763.1 84.2 %copy-start.88 = (f32[1152]{0:T(1024)S(1)}, f32[1152]{0:T(1024)}, u32[]{:S(2)}) copy-start(f32[1152]{0:T(1024)} %get-tuple-element.67) | copy-start | bytes 13828
  763.2 150.9 %all-gather.36.cloned.1.call-start = ((), (), s32[]{:S(2)}) async-start(), calls=%async_computation.26 | async-start | bytes 2949120 | tf_op jit(solution)/shard_map/all_gather | solution.py:112
  863.4 90.2 %all-gather.56.cloned.1.call-start = ((), (), s32[]{:S(2)}) async-start(), calls=%async_computation.47 | async-start | bytes 3981312 | tf_op jit(solution)/shard_map/all_gather | solution.py:96
  864.0 130.4 %all-gather.58.cloned.1.call-start = ((), (), s32[]{:S(2)}) async-start(), calls=%async_computation.48 | async-start | bytes 3981312 | tf_op jit(solution)/shard_map/all_gather | solution.py:97
  864.6 181.9 %all-gather.60.cloned.1.call-start = ((), (), s32[]{:S(2)}) async-start(), calls=%async_computation.49 | async-start | bytes 2949120 | tf_op jit(solution)/shard_map/all_gather | solution.py:116
  866.7 266.0 %reduce-scatter.39.cloned.1.call-start = ((), (), s32[]{:S(2)}) async-start(), calls=%async_computation.27 | async-start | bytes 5898240 | tf_op jit(solution)/shard_map/reduce_scatter | solution.py:120
  918.1 35.6 %copy-start.125 = (f32[1152]{0:T(1024)S(1)}, f32[1152]{0:T(1024)}, u32[]{:S(2)}) copy-start(f32[1152]{0:T(1024)} %get-tuple-element.65) | copy-start | bytes 13828
  1004.0 217.3 %reduce-scatter.41.cloned.1.call-start = ((), (), s32[]{:S(2)}) async-start(), calls=%async_computation.28 | async-start | bytes 5898240 | tf_op jit(solution)/shard_map/reduce_scatter | solution.py:126
  1071.2 219.5 %all-gather.62.cloned.1.call-start = ((), (), s32[]{:S(2)}) async-start(), calls=%async_computation.50 | async-start | bytes 2949120 | tf_op jit(solution)/shard_map/all_gather | solution.py:116
  1073.7 59.0 %copy-start.107 = (f32[1152]{0:T(1024)S(1)}, f32[1152]{0:T(1024)}, u32[]{:S(2)}) copy-start(f32[1152]{0:T(1024)} %get-tuple-element.63) | copy-start | bytes 13828
  1240.0 180.7 %reduce-scatter.43.cloned.1.call-start = ((), (), s32[]{:S(2)}) async-start(), calls=%async_computation.29 | async-start | bytes 5898240 | tf_op jit(solution)/shard_map/reduce_scatter | solution.py:126
  1336.5 86.9 %copy-start.3 = (f32[1,4,4,4,4,1152]{5,2,1,4,3,0:T(4,128)S(1)}, f32[1,4,4,4,4,1152]{5,2,1,4,3,0:T(4,128)}, u32[]{:S(2)}) copy-start(f32[1,4,4,4,4,1152]{5,2,1,4,3,0:T(4,128)} %copy-done.2) | copy-start | bytes 3538948
  1336.5 166.6 %all-gather.38.cloned.1.call-start = ((), (), s32[]{:S(2)}) async-start(), calls=%async_computation.30 | async-start | bytes 2949120 | tf_op jit(solution)/shard_map/all_gather | solution.py:116
  1453.3 150.2 %reduce-scatter.45.cloned.1.call-start = ((), (), s32[]{:S(2)}) async-start(), calls=%async_computation.31 | async-start | bytes 5898240 | tf_op jit(solution)/shard_map/reduce_scatter | solution.py:126
  1519.4 84.2 %copy-start.65 = (f32[4,4,16]{2,1,0:T(4,128)S(1)}, f32[4,4,16]{2,1,0:T(4,128)}, u32[]{:S(2)}) copy-start(f32[4,4,16]{2,1,0:T(4,128)} %copy-done.64) | copy-start | bytes 3076
  1519.4 84.2 %copy-start.70 = (f32[1152]{0:T(1024)S(1)}, f32[1152]{0:T(1024)}, u32[]{:S(2)}) copy-start(f32[1152]{0:T(1024)} %copy-done.69) | copy-start | bytes 13828
  1519.4 142.4 %all-gather.64.cloned.1.call-start = ((), (), s32[]{:S(2)}) async-start(), calls=%async_computation.51 | async-start | bytes 2949120 | tf_op jit(solution)/shard_map/all_gather | solution.py:116
  1609.2 52.6 %copy-start.43 = (bf16[1,288,1152]{2,1,0:T(8,128)(2,1)S(1)}, bf16[1,288,1152]{2,1,0:T(8,128)(2,1)}, u32[]{:S(2)}) copy-start(bf16[1,288,1152]{2,1,0:T(8,128)(2,1)} %copy.239) | copy-start | bytes 1990660
  1611.1 185.7 %reduce-scatter.47.cloned.1.call-start = ((), (), s32[]{:S(2)}) async-start(), calls=%async_computation.32 | async-start | bytes 5898240 | tf_op jit(solution)/shard_map/reduce_scatter | solution.py:126
  1712.6 172.3 %reduce-scatter.63.cloned.1.call-start = ((), (), s32[]{:S(2)}) async-start(), calls=%async_computation.53 | async-start | bytes 4423680 | tf_op jit(solution)/shard_map/reshape.137
  1715.7 219.9 %reduce-scatter.61.cloned.1.call-start = ((), (), s32[]{:S(2)}) async-start(), calls=%async_computation.52 | async-start | bytes 4423680 | tf_op jit(solution)/shard_map/reshape.135
  1717.2 79.6 %copy-start.9 = (bf16[1,4,4,16,1152]{4,3,2,1,0:T(8,128)(2,1)S(1)}, bf16[1,4,4,16,1152]{4,3,2,1,0:T(8,128)(2,1)}, u32[]{:S(2)}) copy-start(bf16[1,4,4,16,1152]{4,3,2,1,0:T(8,128)(2,1)} %param.13) | copy-start | bytes 1769476
  1717.2 79.6 %copy-start.63 = (f32[4,4,16]{2,1,0:T(4,128)S(1)}, f32[4,4,16]{2,1,0:T(4,128)}, u32[]{:S(2)}) copy-start(f32[4,4,16]{2,1,0:T(4,128)} %copy-done.62) | copy-start | bytes 3076
  1717.2 79.6 %copy-start.68 = (f32[1152]{0:T(1024)S(1)}, f32[1152]{0:T(1024)}, u32[]{:S(2)}) copy-start(f32[1152]{0:T(1024)} %copy-done.67) | copy-start | bytes 13828
  1717.2 81.3 %copy-start.97 = (f32[4,4,16]{2,1,0:T(4,128)S(1)}, f32[4,4,16]{2,1,0:T(4,128)}, u32[]{:S(2)}) copy-start(f32[4,4,16]{2,1,0:T(4,128)} %copy-done.96) | copy-start | bytes 3076
  1719.5 79.2 %copy-start.75 = (f32[4,4,16]{2,1,0:T(4,128)S(1)}, f32[4,4,16]{2,1,0:T(4,128)}, u32[]{:S(2)}) copy-start(f32[4,4,16]{2,1,0:T(4,128)} %copy-done.74) | copy-start | bytes 3076
  1802.4 154.7 %reduce-scatter.71.cloned.1.call-start = ((), (), s32[]{:S(2)}) async-start(), calls=%async_computation.57 | async-start | bytes 1327104
  1807.3 183.6 %reduce-scatter.67.cloned.1.call-start = ((), (), s32[]{:S(2)}) async-start(), calls=%async_computation.55 | async-start | bytes 3096576
  1827.9 183.9 %reduce-scatter.69.cloned.1.call-start = ((), (), s32[]{:S(2)}) async-start(), calls=%async_computation.56 | async-start | bytes 1327104
  1832.9 212.6 %reduce-scatter.65.cloned.1.call-start = ((), (), s32[]{:S(2)}) async-start(), calls=%async_computation.54 | async-start | bytes 3096576
  1853.5 233.0 %reduce-scatter.55.cloned.1.call-start = ((), (), s32[]{:S(2)}) async-start(), calls=%async_computation.36 | async-start | bytes 3981312 | tf_op jit(solution)/shard_map/reduce_scatter | solution.py:142
  1860.7 266.0 %reduce-scatter.59.cloned.1.call-start = ((), (), s32[]{:S(2)}) async-start(), calls=%async_computation.38 | async-start | bytes 3981312 | tf_op jit(solution)/shard_map/reduce_scatter | solution.py:145
  1868.8 298.1 %reduce-scatter.57.cloned.1.call-start = ((), (), s32[]{:S(2)}) async-start(), calls=%async_computation.37 | async-start | bytes 3981312 | tf_op jit(solution)/shard_map/reduce_scatter | solution.py:145
  1877.0 330.8 %reduce-scatter.53.cloned.1.call-start = ((), (), s32[]{:S(2)}) async-start(), calls=%async_computation.35 | async-start | bytes 3981312 | tf_op jit(solution)/shard_map/reduce_scatter | solution.py:142
  1884.2 380.2 %reduce-scatter.49.cloned.1.call-start = ((), (), s32[]{:S(2)}) async-start(), calls=%async_computation.33 | async-start | bytes 6193152 | tf_op jit(solution)/shard_map/reduce_scatter | solution.py:133
  1943.2 377.6 %reduce-scatter.51.cloned.1.call-start = ((), (), s32[]{:S(2)}) async-start(), calls=%async_computation.34 | async-start | bytes 6193152 | tf_op jit(solution)/shard_map/reduce_scatter | solution.py:133
  1943.8 600.5 %all-reduce.7.cloned.1.call-start = ((), (), s32[]{:S(2)}) async-start(), calls=%async_computation.58 | async-start | bytes 24772608 | tf_op jit(solution)/shard_map/psum | solution.py:150
  2342.4 65.9 %copy-start.93 = (bf16[1,1152]{1,0:T(2,128)(2,1)S(1)}, bf16[1,1152]{1,0:T(2,128)(2,1)}, u32[]{:S(2)}) copy-start(bf16[1,1152]{1,0:T(2,128)(2,1)} %param.14) | copy-start | bytes 6916
  2342.4 65.9 %copy-start.95 = (f32[1,1152]{1,0:T(1,128)S(1)}, f32[1,1152]{1,0:T(1,128)}, u32[]{:S(2)}) copy-start(f32[1,1152]{1,0:T(1,128)} %copy-done.94) | copy-start | bytes 13828
  (111 other events, 329.5 us)
Sparse Core Ops, SparseCore 0:
  11.8 58.6 all-gather.39
  72.7 55.9 all-gather.51
  130.8 68.2 all-gather.43
  201.2 49.9 all-gather.41
  285.5 84.0 reduce-scatter.32
  371.5 39.8 all-gather.47
  413.6 49.9 all-gather.45
  465.7 38.1 all-gather.49
  513.6 85.2 reduce-scatter.34
  600.9 68.7 all-gather.53
  671.8 50.0 all-gather.33
  763.3 84.0 reduce-scatter.36
  863.6 50.5 all-gather.35
  915.5 38.1 all-gather.55
  955.1 39.3 all-gather.57
  996.5 49.9 all-gather.59
  1048.6 84.0 reduce-scatter.38
  1135.4 85.7 reduce-scatter.40
  1240.2 50.4 all-gather.61
  1336.6 84.0 reduce-scatter.42
  1453.5 49.5 all-gather.37
  1519.5 84.0 reduce-scatter.44
  1611.2 50.4 all-gather.63
  1712.7 84.0 reduce-scatter.46
  1799.1 67.0 reduce-scatter.62
  1868.9 66.6 reduce-scatter.60
  1938.3 18.7 reduce-scatter.70
  1959.4 31.5 reduce-scatter.66
  1993.2 18.5 reduce-scatter.68
  2014.0 31.5 reduce-scatter.64
  2048.4 38.0 reduce-scatter.54
  2088.7 38.0 reduce-scatter.58
  2128.8 38.0 reduce-scatter.56
  2169.7 38.0 reduce-scatter.52
  2210.7 53.6 reduce-scatter.48
  2267.1 53.6 reduce-scatter.50
  2324.8 219.4 all-reduce.6
where the time goes:
time: 2580 us; the launch traced here: 2570 us
  waiting for transfers between devices  1790 us (69%)
  local copies, waits for them, and re-layouts  290 us (11%)
  matrix products  183 us (7%)
  blocking collectives  174 us (7%)
  other arithmetic  106 us (4%)
    reduce_scatter x4, waiting for transfers between devices, reduce_grads(): lax.psum_scatter(term(jnp.int32(0), own_rows * lax.axis_size('tp')), 'tp'...  326 us
    reduce_scatter x4, waiting for transfers between devices, reduce_rows(): lax.psum_scatter(term(jnp.int32(0), own_rows * lax.axis_size('tp')), 'tp'...  298 us
    all_gather x4, waiting for transfers between devices, spread_grads(): return lax.all_gather(values[None], 'tp', axis=0, tiled=True)  192 us
    all_gather x4, waiting for transfers between devices, spread_rows(): return lax.all_gather(values[None], 'tp', axis=0, tiled=True)  184 us
    psum x1, waiting for transfers between devices, sum_weight_grads(): lax.psum(summed[0].astype(jnp.bfloat16), 'ctx').astype(jnp.float32)  135 us
    reduce_scatter x2, waiting for transfers between devices, sum_weight_grads(): lax.psum_scatter(grads[0].astype(jnp.bfloat16), 'shard', scatter_dimensio...  113 us
    all_gather x2, waiting for transfers between devices, fetch_forward(): lax.all_gather(w_ada[number], 'shard', axis=0, tiled=True)  106 us
    unnamed x41, waiting for transfers between devices  93.9 us
  transfers between devices with their start and end apart: 38, of which 35 were waited for; matrix products, arithmetic and copies ran while one was open for 11% of the time, Pallas kernels for 0%

commit v1 on v0

--- a/solution.py
+++ b/solution.py
@@ -147,7 +147,7 @@
         ).astype(jnp.float32),
     )
     return (
-        lax.psum(summed[0].astype(jnp.bfloat16), "ctx").astype(jnp.float32),
+        jnp.sum(lax.all_gather(summed[0].astype(jnp.bfloat16), "ctx"), axis=0).astype(jnp.float32),
         lax.psum(summed[1].astype(jnp.bfloat16), "ctx").astype(jnp.float32),
         lax.psum(summed[2].astype(jnp.bfloat16), "ctx").astype(jnp.float32),
         lax.psum(summed[3].astype(jnp.bfloat16), "ctx").astype(jnp.float32),

time: 2580 us -> 2620 us (1.016)
  waiting for transfers between devices: 1790 us -> 1830 us
    all_gather x0 -> x2, waiting for transfers between devices: none -> 34.9 us  [sum_weight_grads(): lax.all_gather(summed[0].astype(jnp.bfloat16), 'ctx')]
    unnamed x308 -> x310, local copies, waits for them, and re-layouts: 85.3 us -> 83.8 us
    unnamed x41 -> x43, waiting for transfers between devices: 93.9 us -> 94 us
  transfers between devices with their start and end apart: 38 -> 40, of which waited for: 35 -> 36; matrix products, arithmetic and copies ran while one was open for 11% -> 12% of each run, Pallas kernels for 0% -> 0%
where the time goes in v1:
time: 2620 us; the launch traced here: 2610 us
  waiting for transfers between devices  1830 us (70%)
  local copies, waits for them, and re-layouts  288 us (11%)
  matrix products  184 us (7%)
  blocking collectives  173 us (7%)
  other arithmetic  118 us (5%)
    reduce_scatter x4, waiting for transfers between devices, reduce_grads(): lax.psum_scatter(term(jnp.int32(0), own_rows * lax.axis_size('tp')), 'tp'...  326 us
    reduce_scatter x4, waiting for transfers between devices, reduce_rows(): lax.psum_scatter(term(jnp.int32(0), own_rows * lax.axis_size('tp')), 'tp'...  298 us
    all_gather x4, waiting for transfers between devices, spread_grads(): return lax.all_gather(values[None], 'tp', axis=0, tiled=True)  192 us
    all_gather x4, waiting for transfers between devices, spread_rows(): return lax.all_gather(values[None], 'tp', axis=0, tiled=True)  184 us
    psum x1, waiting for transfers between devices, sum_weight_grads(): lax.psum(summed[1].astype(jnp.bfloat16), 'ctx').astype(jnp.float32)  137 us
    reduce_scatter x2, waiting for transfers between devices, sum_weight_grads(): lax.psum_scatter(grads[0].astype(jnp.bfloat16), 'shard', scatter_dimensio...  113 us
    all_gather x2, waiting for transfers between devices, fetch_forward(): lax.all_gather(w_ada[number], 'shard', axis=0, tiled=True)  106 us
    unnamed x43, waiting for transfers between devices  94 us
  transfers between devices with their start and end apart: 40, of which 36 were waited for; matrix products, arithmetic and copies ran while one was open for 12% of the time, Pallas kernels for 0%

profile of v1, /device:TPU:0, one launch (start us, length us, event | category | flops | bytes accessed | tf_op | source)
XLA Modules:
  0.0 2613.7 jit_solution(6448307303717405108)
XLA Ops:
  20.1 50.5 %all-gather.44.cloned.1.call-done = bf16[1,1152,1728]{2,1,0:T(8,128)(2,1)} async-done(((bf16[1,576,1728]{2,1,0:T(8,128)(2,1)}), bf16[1,1152,1728]{2,1,0:T(8,128)(2,1)}) %all-gather.44.cloned.1.call-update) | async-done | bytes 3981328 | tf_op jit(solution)/shard_map/all_gather | solution.py:93
  73.6 55.1 %all-gather.56.cloned.1.call-done = bf16[1,1152,1728]{2,1,0:T(8,128)(2,1)} async-done(((bf16[1,576,1728]{2,1,0:T(8,128)(2,1)}), bf16[1,1152,1728]{2,1,0:T(8,128)(2,1)}) %all-gather.56.cloned.1.call-update) | async-done | bytes 3981328 | tf_op jit(solution)/shard_map/all_gather | solution.py:93
  131.7 20.4 all-reduce.3
  156.8 40.7 %all-gather.4 = bf16[1,288,1152]{1,0,2:T(2,128)(2,1)S(1)} all-gather(bf16[1,288,576]{1,0,2:T(2,128)(2,1)S(1)} %copy.425), channel_id=6, replica_groups=mesh['shard'=2,'ctx'=4,'tp'=4] {'shard'}, dimensions={2}, use_global_device_ids=true | all-gather | bytes 995328 | tf_op jit(solution)/shard_map/all_gather | solution.py:95
  201.2 7.1 copy.308
  208.3 42.9 %all-gather.46.cloned.1.call-done = bf16[4,4,4,16,1152]{4,3,2,1,0:T(8,128)(2,1)} async-done(((bf16[1,4,4,16,1152]{4,3,2,1,0:T(8,128)(2,1)}), bf16[4,4,4,16,1152]{4,3,2,1,0:T(8,128)(2,1)}) %all-gather.46.cloned.1.call-update) | async-done | bytes 2359312 | tf_op jit(solution)/shard_map/all_gather | solution.py:112
  289.5 80.0 %reduce-scatter.33.cloned.1.call-done = f32[256,1152]{1,0:T(8,128)} async-done(((f32[1024,1152]{1,0:T(8,128)}), f32[256,1152]{1,0:T(8,128)}) %reduce-scatter.33.cloned.1.call-update) | async-done | bytes 1179664 | tf_op jit(solution)/shard_map/reduce_scatter | solution.py:120
  377.5 34.0 %all-gather.52.cloned.1.call-done = bf16[1,1152,1152]{2,1,0:T(8,128)(2,1)} async-done(((bf16[1,576,1152]{2,1,0:T(8,128)(2,1)}), bf16[1,1152,1152]{2,1,0:T(8,128)(2,1)}) %all-gather.52.cloned.1.call-update) | async-done | bytes 2654224 | tf_op jit(solution)/shard_map/all_gather | solution.py:96
  411.5 52.2 %all-gather.50.cloned.1.call-done = bf16[4,4,4,16,1152]{4,3,2,1,0:T(8,128)(2,1)} async-done(((bf16[1,4,4,16,1152]{4,3,2,1,0:T(8,128)(2,1)}), bf16[4,4,4,16,1152]{4,3,2,1,0:T(8,128)(2,1)}) %all-gather.50.cloned.1.call-update) | async-done | bytes 2359312 | tf_op jit(solution)/shard_map/all_gather | solution.py:112
  463.6 8.1 convolution_add_fusion.1
  471.8 32.1 %all-gather.54.cloned.1.call-done = bf16[1,1152,1152]{1,2,0:T(8,128)(2,1)} async-done(((bf16[1,1152,576]{1,2,0:T(8,128)(2,1)}), bf16[1,1152,1152]{1,2,0:T(8,128)(2,1)}) %all-gather.54.cloned.1.call-update) | async-done | bytes 2654224 | tf_op jit(solution)/shard_map/all_gather | solution.py:97
  503.9 9.6 fusion.37
  518.3 80.6 %reduce-scatter.35.cloned.1.call-done = f32[256,1152]{1,0:T(8,128)} async-done(((f32[1024,1152]{1,0:T(8,128)}), f32[256,1152]{1,0:T(8,128)}) %reduce-scatter.35.cloned.1.call-update) | async-done | bytes 1179664 | tf_op jit(solution)/shard_map/reduce_scatter | solution.py:120
  606.1 8.3 all-to-all-done
  628.0 41.4 %all-gather.11 = bf16[1,288,1152]{1,0,2:T(2,128)(2,1)S(1)} all-gather(bf16[1,288,576]{1,0,2:T(2,128)(2,1)} %copy.427), channel_id=13, replica_groups=mesh['shard'=2,'ctx'=4,'tp'=4] {'shard'}, dimensions={2}, use_global_device_ids=true | all-gather | bytes 995328 | tf_op jit(solution)/shard_map/all_gather | solution.py:95
  673.2 7.1 copy.331
  680.4 41.5 %all-gather.38.cloned.1.call-done = bf16[4,1,16,4,4,1152]{5,2,4,3,1,0:T(8,128)(2,1)} async-done(((bf16[1,1,16,4,4,1152]{5,2,4,3,1,0:T(8,128)(2,1)}), bf16[4,1,16,4,4,1152]{5,2,4,3,1,0:T(8,128)(2,1)}) %all-gather.38.cloned.1.call-update) | async-done | bytes 2359312 | tf_op jit(solution)/shard_map/all_gather | solution.py:112
  763.3 84.2 %reduce-scatter.37.cloned.1.call-done = f32[256,1152]{1,0:T(8,128)} async-done(((f32[1024,1152]{1,0:T(8,128)}), f32[256,1152]{1,0:T(8,128)}) %reduce-scatter.37.cloned.1.call-update) | async-done | bytes 1179664 | tf_op jit(solution)/shard_map/reduce_scatter | solution.py:120
  866.8 47.3 %all-gather.40.cloned.1.call-done = bf16[4,1,16,4,4,1152]{5,2,4,3,1,0:T(8,128)(2,1)} async-done(((bf16[1,1,16,4,4,1152]{5,2,4,3,1,0:T(8,128)(2,1)}), bf16[4,1,16,4,4,1152]{5,2,4,3,1,0:T(8,128)(2,1)}) %all-gather.40.cloned.1.call-update) | async-done | bytes 2359312 | tf_op jit(solution)/shard_map/all_gather | solution.py:112
  923.6 30.1 %all-gather.60.cloned.1.call-done = bf16[1,1152,1152]{2,1,0:T(8,128)(2,1)} async-done(((bf16[1,576,1152]{2,1,0:T(8,128)(2,1)}), bf16[1,1152,1152]{2,1,0:T(8,128)(2,1)}) %all-gather.60.cloned.1.call-update) | async-done | bytes 2654224 | tf_op jit(solution)/shard_map/all_gather | solution.py:96
  953.7 8.1 convolution_add_fusion
  961.9 32.6 %all-gather.62.cloned.1.call-done = bf16[1,1152,1152]{1,2,0:T(8,128)(2,1)} async-done(((bf16[1,1152,576]{1,2,0:T(8,128)(2,1)}), bf16[1,1152,1152]{1,2,0:T(8,128)(2,1)}) %all-gather.62.cloned.1.call-update) | async-done | bytes 2654224 | tf_op jit(solution)/shard_map/all_gather | solution.py:97
  994.5 9.5 fusion.28
  1004.1 42.4 %all-gather.64.cloned.1.call-done = bf16[4,16,4,4,1152]{4,1,3,2,0:T(8,128)(2,1)} async-done(((bf16[1,16,4,4,1152]{4,1,3,2,0:T(8,128)(2,1)}), bf16[4,16,4,4,1152]{4,1,3,2,0:T(8,128)(2,1)}) %all-gather.64.cloned.1.call-update) | async-done | bytes 2359312 | tf_op jit(solution)/shard_map/all_gather | solution.py:116
  1055.5 9.1 convert_reduce_fusion.4
  1079.3 53.5 %reduce-scatter.39.cloned.1.call-done = f32[256,1152]{1,0:T(8,128)} async-done(((f32[1024,1152]{1,0:T(8,128)}), f32[256,1152]{1,0:T(8,128)}) %reduce-scatter.39.cloned.1.call-update) | async-done | bytes 1179664 | tf_op jit(solution)/shard_map/reduce_scatter | solution.py:120
  1137.7 83.6 %reduce-scatter.41.cloned.1.call-done = f32[256,1152]{1,0:T(8,128)} async-done(((f32[1024,1152]{1,0:T(8,128)}), f32[256,1152]{1,0:T(8,128)}) %reduce-scatter.41.cloned.1.call-update) | async-done | bytes 1179664 | tf_op jit(solution)/shard_map/reduce_scatter | solution.py:126
  1241.1 49.7 %all-gather.66.cloned.1.call-done = bf16[4,16,4,4,1152]{4,1,3,2,0:T(8,128)(2,1)} async-done(((bf16[1,16,4,4,1152]{4,1,3,2,0:T(8,128)(2,1)}), bf16[4,16,4,4,1152]{4,1,3,2,0:T(8,128)(2,1)}) %all-gather.66.cloned.1.call-update) | async-done | bytes 2359312 | tf_op jit(solution)/shard_map/all_gather | solution.py:116
  1329.3 7.2 convolution_bitcast_fusion.1
  1338.1 82.7 %reduce-scatter.43.cloned.1.call-done = f32[256,1152]{1,0:T(8,128)} async-done(((f32[1024,1152]{1,0:T(8,128)}), f32[256,1152]{1,0:T(8,128)}) %reduce-scatter.43.cloned.1.call-update) | async-done | bytes 1179664 | tf_op jit(solution)/shard_map/reduce_scatter | solution.py:126
  1439.7 12.1 all_to_all.8
  1453.4 49.7 %all-gather.42.cloned.1.call-done = bf16[4,1,4,4,16,1152]{5,4,3,2,1,0:T(8,128)(2,1)} async-done(((bf16[1,1,4,4,16,1152]{5,4,3,2,1,0:T(8,128)(2,1)}), bf16[4,1,4,4,16,1152]{5,4,3,2,1,0:T(8,128)(2,1)}) %all-gather.42.cloned.1.call-update) | async-done | bytes 2359312 | tf_op jit(solution)/shard_map/all_gather | solution.py:116
  1503.1 9.6 convert_reduce_fusion.5
  1520.8 82.7 %reduce-scatter.45.cloned.1.call-done = f32[256,1152]{1,0:T(8,128)} async-done(((f32[1024,1152]{1,0:T(8,128)}), f32[256,1152]{1,0:T(8,128)}) %reduce-scatter.45.cloned.1.call-update) | async-done | bytes 1179664 | tf_op jit(solution)/shard_map/reduce_scatter | solution.py:126
  1611.1 50.6 %all-gather.68.cloned.1.call-done = bf16[4,4,4,16,1152]{4,3,2,1,0:T(8,128)(2,1)} async-done(((bf16[1,4,4,16,1152]{4,3,2,1,0:T(8,128)(2,1)}), bf16[4,4,4,16,1152]{4,3,2,1,0:T(8,128)(2,1)}) %all-gather.68.cloned.1.call-update) | async-done | bytes 2359312 | tf_op jit(solution)/shard_map/all_gather | solution.py:116
  1705.2 7.2 convolution_bitcast_fusion
  1719.5 77.2 %reduce-scatter.47.cloned.1.call-done = f32[256,1152]{1,0:T(8,128)} async-done(((f32[1024,1152]{1,0:T(8,128)}), f32[256,1152]{1,0:T(8,128)}) %reduce-scatter.47.cloned.1.call-update) | async-done | bytes 1179664 | tf_op jit(solution)/shard_map/reduce_scatter | solution.py:126
  1813.1 7.2 copy.416
  1820.3 7.5 reshape.1256
  1838.7 7.2 copy.414
  1845.9 7.4 reshape.1254
  1853.4 7.1 convolution_convert_fusion.2
  1860.6 8.0 convolution_convert_fusion
  1868.9 8.0 convolution_convert_fusion.1
  1877.0 7.1 convolution_convert_fusion.3
  1886.3 49.2 %reduce-scatter.61.cloned.1.call-done = f32[1728,1]{1,0:T(8,128)} async-done(((f32[6912,1]{1,0:T(8,128)}), f32[1728,1]{1,0:T(8,128)}) %reduce-scatter.61.cloned.1.call-update) | async-done | bytes 6928 | tf_op jit(solution)/shard_map/reshape.135
  1937.0 6.1 multiply_convert_fusion.1
  1943.8 13.3 reduce-scatter.71.cloned.1.call-done
  1958.9 31.9 %reduce-scatter.67.cloned.1.call-done = bf16[576,864]{1,0:T(8,128)(2,1)} async-done(((bf16[1152,864]{1,0:T(8,128)(2,1)}), bf16[576,864]{1,0:T(8,128)(2,1)}) %reduce-scatter.67.cloned.1.call-update) | async-done | bytes 995344
  1997.6 14.2 reduce-scatter.69.cloned.1.call-done
  2013.7 31.8 %reduce-scatter.65.cloned.1.call-done = bf16[576,864]{1,0:T(8,128)(2,1)} async-done(((bf16[1152,864]{1,0:T(8,128)(2,1)}), bf16[576,864]{1,0:T(8,128)(2,1)}) %reduce-scatter.65.cloned.1.call-update) | async-done | bytes 995344
  2052.2 34.1 %reduce-scatter.55.cloned.1.call-done = bf16[576,1152]{1,0:T(8,128)(2,1)} async-done(((bf16[1152,1152]{1,0:T(8,128)(2,1)}), bf16[576,1152]{1,0:T(8,128)(2,1)}) %reduce-scatter.55.cloned.1.call-update) | async-done | bytes 1327120 | tf_op jit(solution)/shard_map/reduce_scatter | solution.py:142
  2086.3 40.3 %reduce-scatter.59.cloned.1.call-done = bf16[1152,576]{0,1:T(8,128)(2,1)} async-done(((bf16[1152,1152]{0,1:T(8,128)(2,1)}), bf16[1152,576]{0,1:T(8,128)(2,1)}) %reduce-scatter.59.cloned.1.call-update) | async-done | bytes 1327120 | tf_op jit(solution)/shard_map/reduce_scatter | solution.py:145
  2126.7 40.2 %reduce-scatter.57.cloned.1.call-done = bf16[1152,576]{0,1:T(8,128)(2,1)} async-done(((bf16[1152,1152]{0,1:T(8,128)(2,1)}), bf16[1152,576]{0,1:T(8,128)(2,1)}) %reduce-scatter.57.cloned.1.call-update) | async-done | bytes 1327120 | tf_op jit(solution)/shard_map/reduce_scatter | solution.py:145
  2166.8 40.9 %reduce-scatter.53.cloned.1.call-done = bf16[576,1152]{1,0:T(8,128)(2,1)} async-done(((bf16[1152,1152]{1,0:T(8,128)(2,1)}), bf16[576,1152]{1,0:T(8,128)(2,1)}) %reduce-scatter.53.cloned.1.call-update) | async-done | bytes 1327120 | tf_op jit(solution)/shard_map/reduce_scatter | solution.py:142
  2207.8 56.5 %reduce-scatter.49.cloned.1.call-done = bf16[576,1728]{1,0:T(8,128)(2,1)} async-done(((bf16[1152,1728]{1,0:T(8,128)(2,1)}), bf16[576,1728]{1,0:T(8,128)(2,1)}) %reduce-scatter.49.cloned.1.call-update) | async-done | bytes 1990672 | tf_op jit(solution)/shard_map/reduce_scatter | solution.py:133
  2264.6 56.2 %reduce-scatter.51.cloned.1.call-done = bf16[576,1728]{1,0:T(8,128)(2,1)} async-done(((bf16[1152,1728]{1,0:T(8,128)(2,1)}), bf16[576,1728]{1,0:T(8,128)(2,1)}) %reduce-scatter.51.cloned.1.call-update) | async-done | bytes 1990672 | tf_op jit(solution)/shard_map/reduce_scatter | solution.py:133
  2328.3 6.9 fusion.111
  2338.1 137.1 %all-reduce.7.cloned.1.call-done = (bf16[1,3,576,288]{2,3,1,0:T(8,128)(2,1)}, bf16[1,3,576,288]{2,3,1,0:T(8,128)(2,1)}, bf16[1,288,576]{2,1,0:T(8,128)(2,1)}, bf...) async-done(((bf16[1,3,576,288]{2,3,1,0:T(8,128)(2,1)}, ...) | async-done | bytes 7962640 | tf_op jit(solution)/shard_map/psum | solution.py:151
  2488.3 6.3 fusion.108
  2494.6 34.5 %psum.98 = f32[1,1152]{1,0:T(1,128)S(1)} all-reduce(f32[1,1152]{1,0:T(1,128)S(1)} %add.583), channel_id=1, replica_groups=mesh['shard'=2,'ctx'=4,'tp'=4] {'ctx','tp'}, use_global_device_ids=true, to_apply=%region_44.45 | all-reduce | flops 1152 | bytes 9216 | tf_op jit(solution)/shard_map/psum | solution.py:371
  2529.2 23.9 all-reduce.2
  2559.7 34.9 %all-gather.72.cloned.1.call-done = bf16[2304,1728]{1,0:T(8,128)(2,1)} async-done(((bf16[576,1728]{1,0:T(8,128)(2,1)}), bf16[2304,1728]{1,0:T(8,128)(2,1)}) %all-gather.72.cloned.1.call-update) | async-done | bytes 7962640 | tf_op jit(solution)/shard_map/all_gather | solution.py:150
  2594.6 6.6 reduce_sum.555
  (638 shorter events, 431.1 us)
Async XLA Ops:
  7.2 63.4 %all-gather.44.cloned.1.call-start = ((), (), s32[]{:S(2)}) async-start(), calls=%async_computation.39 | async-start | bytes 6193152 | tf_op jit(solution)/shard_map/all_gather | solution.py:93
  11.7 117.0 %all-gather.56.cloned.1.call-start = ((), (), s32[]{:S(2)}) async-start(), calls=%async_computation.45 | async-start | bytes 6193152 | tf_op jit(solution)/shard_map/all_gather | solution.py:93
  12.5 188.8 %all-gather.48.cloned.1.call-start = ((), (), s32[]{:S(2)}) async-start(), calls=%async_computation.41 | async-start | bytes 5308416 | tf_op jit(solution)/shard_map/all_gather | solution.py:94
  17.4 233.7 %all-gather.46.cloned.1.call-start = ((), (), s32[]{:S(2)}) async-start(), calls=%async_computation.40 | async-start | bytes 2949120 | tf_op jit(solution)/shard_map/all_gather | solution.py:112
  17.7 135.0 %copy-start.63 = (f32[4,4,16]{2,1,0:T(4,128)}, f32[4,4,16]{2,1,0:T(4,128)S(1)}, u32[]{:S(2)}) copy-start(f32[4,4,16]{2,1,0:T(4,128)S(1)} %broadcast_multiply_fusion.3) | copy-start | bytes 3076
  18.1 55.3 %copy-start.97 = (f32[4,4,16]{2,1,0:T(4,128)}, f32[4,4,16]{2,1,0:T(4,128)S(1)}, u32[]{:S(2)}) copy-start(f32[4,4,16]{2,1,0:T(4,128)S(1)} %fusion.84) | copy-start | bytes 3076
  18.7 110.0 %copy-start.95 = (f32[1,1152]{1,0:T(1,128)}, f32[1,1152]{1,0:T(1,128)S(1)}, u32[]{:S(2)}) copy-start(f32[1,1152]{1,0:T(1,128)S(1)} %get-tuple-element.102) | copy-start | bytes 13828
  20.0 132.7 %copy-start.75 = (f32[4,4,16]{2,1,0:T(4,128)}, f32[4,4,16]{2,1,0:T(4,128)S(1)}, u32[]{:S(2)}) copy-start(f32[4,4,16]{2,1,0:T(4,128)S(1)} %fusion.129) | copy-start | bytes 3076
  73.5 80.4 %copy-start.125 = (bf16[2,2,288]{2,1,0:T(2,128)(2,1)S(1)}, bf16[2,2,288]{2,1,0:T(2,128)(2,1)}, u32[]{:S(2)}) copy-start(bf16[2,2,288]{2,1,0:T(2,128)(2,1)} %param.18) | copy-start | bytes 6916
  73.5 81.1 %copy-start.57 = (bf16[2,288,576]{2,1,0:T(8,128)(2,1)S(1)}, bf16[2,288,576]{2,1,0:T(8,128)(2,1)}, u32[]{:S(2)}) copy-start(bf16[2,288,576]{2,1,0:T(8,128)(2,1)} %param.19) | copy-start | bytes 1990660
  152.7 218.2 %copy-start.80 = (f32[1152]{0:T(1024)}, f32[1152]{0:T(1024)S(1)}, u32[]{:S(2)}) copy-start(f32[1152]{0:T(1024)S(1)} %get-tuple-element.73) | copy-start | bytes 13828
  152.7 219.4 %copy-start.70 = (f32[1152]{0:T(1024)}, f32[1152]{0:T(1024)S(1)}, u32[]{:S(2)}) copy-start(f32[1152]{0:T(1024)S(1)} %get-tuple-element.70) | copy-start | bytes 13828
  153.8 215.7 %reduce-scatter.33.cloned.1.call-start = ((), (), s32[]{:S(2)}) async-start(), calls=%async_computation.22 | async-start | bytes 5898240 | tf_op jit(solution)/shard_map/reduce_scatter | solution.py:120
  285.4 126.1 %all-gather.52.cloned.1.call-start = ((), (), s32[]{:S(2)}) async-start(), calls=%async_computation.43 | async-start | bytes 3981312 | tf_op jit(solution)/shard_map/all_gather | solution.py:96
  288.9 174.8 %all-gather.50.cloned.1.call-start = ((), (), s32[]{:S(2)}) async-start(), calls=%async_computation.42 | async-start | bytes 2949120 | tf_op jit(solution)/shard_map/all_gather | solution.py:112
  289.5 81.4 %copy-start.86 = (f32[1152]{0:T(1024)}, f32[1152]{0:T(1024)S(1)}, u32[]{:S(2)}) copy-start(f32[1152]{0:T(1024)S(1)} %get-tuple-element.81) | copy-start | bytes 13828
  373.2 130.7 %all-gather.54.cloned.1.call-start = ((), (), s32[]{:S(2)}) async-start(), calls=%async_computation.44 | async-start | bytes 3981312 | tf_op jit(solution)/shard_map/all_gather | solution.py:97
  376.8 222.1 %reduce-scatter.35.cloned.1.call-start = ((), (), s32[]{:S(2)}) async-start(), calls=%async_computation.23 | async-start | bytes 5898240 | tf_op jit(solution)/shard_map/reduce_scatter | solution.py:120
  513.5 159.7 %all-gather.58.cloned.1.call-start = ((), (), s32[]{:S(2)}) async-start(), calls=%async_computation.46 | async-start | bytes 5308416 | tf_op jit(solution)/shard_map/all_gather | solution.py:94
  517.6 82.6 %copy-start.82 = (f32[1152]{0:T(1024)S(1)}, f32[1152]{0:T(1024)}, u32[]{:S(2)}) copy-start(f32[1152]{0:T(1024)} %get-tuple-element.68) | copy-start | bytes 13828
  518.3 82.2 %copy-start.84 = (f32[1152]{0:T(1024)}, f32[1152]{0:T(1024)S(1)}, u32[]{:S(2)}) copy-start(f32[1152]{0:T(1024)S(1)} %get-tuple-element.77) | copy-start | bytes 13828
  601.5 13.0 all-to-all-start
  605.0 116.9 %all-gather.38.cloned.1.call-start = ((), (), s32[]{:S(2)}) async-start(), calls=%async_computation.24 | async-start | bytes 2949120 | tf_op jit(solution)/shard_map/all_gather | solution.py:112
  624.7 222.7 %reduce-scatter.37.cloned.1.call-start = ((), (), s32[]{:S(2)}) async-start(), calls=%async_computation.25 | async-start | bytes 5898240 | tf_op jit(solution)/shard_map/reduce_scatter | solution.py:120
  763.2 84.2 %copy-start.91 = (f32[1152]{0:T(1024)S(1)}, f32[1152]{0:T(1024)}, u32[]{:S(2)}) copy-start(f32[1152]{0:T(1024)} %get-tuple-element.80) | copy-start | bytes 13828
  763.2 150.9 %all-gather.40.cloned.1.call-start = ((), (), s32[]{:S(2)}) async-start(), calls=%async_computation.26 | async-start | bytes 2949120 | tf_op jit(solution)/shard_map/all_gather | solution.py:112
  863.5 90.2 %all-gather.60.cloned.1.call-start = ((), (), s32[]{:S(2)}) async-start(), calls=%async_computation.47 | async-start | bytes 3981312 | tf_op jit(solution)/shard_map/all_gather | solution.py:96
  864.1 130.4 %all-gather.62.cloned.1.call-start = ((), (), s32[]{:S(2)}) async-start(), calls=%async_computation.48 | async-start | bytes 3981312 | tf_op jit(solution)/shard_map/all_gather | solution.py:97
  864.7 181.8 %all-gather.64.cloned.1.call-start = ((), (), s32[]{:S(2)}) async-start(), calls=%async_computation.49 | async-start | bytes 2949120 | tf_op jit(solution)/shard_map/all_gather | solution.py:116
  866.8 266.0 %reduce-scatter.39.cloned.1.call-start = ((), (), s32[]{:S(2)}) async-start(), calls=%async_computation.27 | async-start | bytes 5898240 | tf_op jit(solution)/shard_map/reduce_scatter | solution.py:120
  1004.0 217.3 %reduce-scatter.41.cloned.1.call-start = ((), (), s32[]{:S(2)}) async-start(), calls=%async_computation.28 | async-start | bytes 5898240 | tf_op jit(solution)/shard_map/reduce_scatter | solution.py:126
  1071.2 219.5 %all-gather.66.cloned.1.call-start = ((), (), s32[]{:S(2)}) async-start(), calls=%async_computation.50 | async-start | bytes 2949120 | tf_op jit(solution)/shard_map/all_gather | solution.py:116
  1073.8 59.0 %copy-start.108 = (f32[1152]{0:T(1024)S(1)}, f32[1152]{0:T(1024)}, u32[]{:S(2)}) copy-start(f32[1152]{0:T(1024)} %get-tuple-element.76) | copy-start | bytes 13828
  1240.1 180.7 %reduce-scatter.43.cloned.1.call-start = ((), (), s32[]{:S(2)}) async-start(), calls=%async_computation.29 | async-start | bytes 5898240 | tf_op jit(solution)/shard_map/reduce_scatter | solution.py:126
  1336.5 86.9 %copy-start.3 = (f32[1,4,4,4,4,1152]{5,2,1,4,3,0:T(4,128)S(1)}, f32[1,4,4,4,4,1152]{5,2,1,4,3,0:T(4,128)}, u32[]{:S(2)}) copy-start(f32[1,4,4,4,4,1152]{5,2,1,4,3,0:T(4,128)} %copy-done.2) | copy-start | bytes 3538948
  1336.6 166.5 %all-gather.42.cloned.1.call-start = ((), (), s32[]{:S(2)}) async-start(), calls=%async_computation.30 | async-start | bytes 2949120 | tf_op jit(solution)/shard_map/all_gather | solution.py:116
  1453.3 150.2 %reduce-scatter.45.cloned.1.call-start = ((), (), s32[]{:S(2)}) async-start(), calls=%async_computation.31 | async-start | bytes 5898240 | tf_op jit(solution)/shard_map/reduce_scatter | solution.py:126
  1519.3 84.2 %copy-start.66 = (f32[4,4,16]{2,1,0:T(4,128)S(1)}, f32[4,4,16]{2,1,0:T(4,128)}, u32[]{:S(2)}) copy-start(f32[4,4,16]{2,1,0:T(4,128)} %copy-done.65) | copy-start | bytes 3076
  1519.3 84.2 %copy-start.71 = (f32[1152]{0:T(1024)S(1)}, f32[1152]{0:T(1024)}, u32[]{:S(2)}) copy-start(f32[1152]{0:T(1024)} %copy-done.70) | copy-start | bytes 13828
  1519.3 142.4 %all-gather.68.cloned.1.call-start = ((), (), s32[]{:S(2)}) async-start(), calls=%async_computation.51 | async-start | bytes 2949120 | tf_op jit(solution)/shard_map/all_gather | solution.py:116
  1609.1 52.6 %copy-start.45 = (bf16[1,288,1152]{2,1,0:T(8,128)(2,1)S(1)}, bf16[1,288,1152]{2,1,0:T(8,128)(2,1)}, u32[]{:S(2)}) copy-start(bf16[1,288,1152]{2,1,0:T(8,128)(2,1)} %copy.322) | copy-start | bytes 1990660
  1611.1 185.6 %reduce-scatter.47.cloned.1.call-start = ((), (), s32[]{:S(2)}) async-start(), calls=%async_computation.32 | async-start | bytes 5898240 | tf_op jit(solution)/shard_map/reduce_scatter | solution.py:126
  1712.5 172.4 %reduce-scatter.63.cloned.1.call-start = ((), (), s32[]{:S(2)}) async-start(), calls=%async_computation.55 | async-start | bytes 4423680 | tf_op jit(solution)/shard_map/reshape.137
  1715.6 219.9 %reduce-scatter.61.cloned.1.call-start = ((), (), s32[]{:S(2)}) async-start(), calls=%async_computation.54 | async-start | bytes 4423680 | tf_op jit(solution)/shard_map/reshape.135
  1717.1 79.6 %copy-start.9 = (bf16[1,4,4,16,1152]{4,3,2,1,0:T(8,128)(2,1)S(1)}, bf16[1,4,4,16,1152]{4,3,2,1,0:T(8,128)(2,1)}, u32[]{:S(2)}) copy-start(bf16[1,4,4,16,1152]{4,3,2,1,0:T(8,128)(2,1)} %param.13) | copy-start | bytes 1769476
  1717.1 79.6 %copy-start.64 = (f32[4,4,16]{2,1,0:T(4,128)S(1)}, f32[4,4,16]{2,1,0:T(4,128)}, u32[]{:S(2)}) copy-start(f32[4,4,16]{2,1,0:T(4,128)} %copy-done.63) | copy-start | bytes 3076
  1717.1 79.6 %copy-start.69 = (f32[1152]{0:T(1024)S(1)}, f32[1152]{0:T(1024)}, u32[]{:S(2)}) copy-start(f32[1152]{0:T(1024)} %copy-done.68) | copy-start | bytes 13828
  1717.1 81.3 %copy-start.98 = (f32[4,4,16]{2,1,0:T(4,128)S(1)}, f32[4,4,16]{2,1,0:T(4,128)}, u32[]{:S(2)}) copy-start(f32[4,4,16]{2,1,0:T(4,128)} %copy-done.97) | copy-start | bytes 3076
  1719.4 79.2 %copy-start.76 = (f32[4,4,16]{2,1,0:T(4,128)S(1)}, f32[4,4,16]{2,1,0:T(4,128)}, u32[]{:S(2)}) copy-start(f32[4,4,16]{2,1,0:T(4,128)} %copy-done.75) | copy-start | bytes 3076
  1802.3 154.7 %reduce-scatter.71.cloned.1.call-start = ((), (), s32[]{:S(2)}) async-start(), calls=%async_computation.59 | async-start | bytes 1327104
  1807.3 183.6 %reduce-scatter.67.cloned.1.call-start = ((), (), s32[]{:S(2)}) async-start(), calls=%async_computation.57 | async-start | bytes 3096576
  1827.8 184.0 %reduce-scatter.69.cloned.1.call-start = ((), (), s32[]{:S(2)}) async-start(), calls=%async_computation.58 | async-start | bytes 1327104
  1832.9 212.6 %reduce-scatter.65.cloned.1.call-start = ((), (), s32[]{:S(2)}) async-start(), calls=%async_computation.56 | async-start | bytes 3096576
  1853.4 233.0 %reduce-scatter.55.cloned.1.call-start = ((), (), s32[]{:S(2)}) async-start(), calls=%async_computation.36 | async-start | bytes 3981312 | tf_op jit(solution)/shard_map/reduce_scatter | solution.py:142
  1860.6 266.1 %reduce-scatter.59.cloned.1.call-start = ((), (), s32[]{:S(2)}) async-start(), calls=%async_computation.38 | async-start | bytes 3981312 | tf_op jit(solution)/shard_map/reduce_scatter | solution.py:145
  1868.7 298.1 %reduce-scatter.57.cloned.1.call-start = ((), (), s32[]{:S(2)}) async-start(), calls=%async_computation.37 | async-start | bytes 3981312 | tf_op jit(solution)/shard_map/reduce_scatter | solution.py:145
  1877.0 330.7 %reduce-scatter.53.cloned.1.call-start = ((), (), s32[]{:S(2)}) async-start(), calls=%async_computation.35 | async-start | bytes 3981312 | tf_op jit(solution)/shard_map/reduce_scatter | solution.py:142
  1884.2 380.1 %reduce-scatter.49.cloned.1.call-start = ((), (), s32[]{:S(2)}) async-start(), calls=%async_computation.33 | async-start | bytes 6193152 | tf_op jit(solution)/shard_map/reduce_scatter | solution.py:133
  1943.1 377.6 %reduce-scatter.51.cloned.1.call-start = ((), (), s32[]{:S(2)}) async-start(), calls=%async_computation.34 | async-start | bytes 6193152 | tf_op jit(solution)/shard_map/reduce_scatter | solution.py:133
  1943.7 531.5 %all-reduce.7.cloned.1.call-start = ((), (), s32[]{:S(2)}) async-start(), calls=%async_computation.60 | async-start | bytes 16515072 | tf_op jit(solution)/shard_map/psum | solution.py:151
  2207.7 345.9 %all-gather.70.cloned.1.call-start = ((), (), s32[]{:S(2)}) async-start(), calls=%async_computation.52 | async-start | bytes 10321920 | tf_op jit(solution)/shard_map/all_gather | solution.py:150
  2264.3 330.3 %all-gather.72.cloned.1.call-start = ((), (), s32[]{:S(2)}) async-start(), calls=%async_computation.53 | async-start | bytes 10321920 | tf_op jit(solution)/shard_map/all_gather | solution.py:150
  2488.3 64.8 %copy-start.94 = (bf16[1,1152]{1,0:T(2,128)(2,1)S(1)}, bf16[1,1152]{1,0:T(2,128)(2,1)}, u32[]{:S(2)}) copy-start(bf16[1,1152]{1,0:T(2,128)(2,1)} %param.14) | copy-start | bytes 6916
  2488.3 64.8 %copy-start.96 = (f32[1,1152]{1,0:T(1,128)S(1)}, f32[1,1152]{1,0:T(1,128)}, u32[]{:S(2)}) copy-start(f32[1,1152]{1,0:T(1,128)} %copy-done.95) | copy-start | bytes 13828
  (114 other events, 379.2 us)
Sparse Core Ops, SparseCore 0:
  11.8 58.6 all-gather.43
  72.7 55.9 all-gather.55
  130.8 68.2 all-gather.47
  201.2 49.9 all-gather.45
  285.5 84.0 reduce-scatter.32
  371.5 39.8 all-gather.51
  413.6 49.9 all-gather.49
  465.7 38.1 all-gather.53
  513.6 85.2 reduce-scatter.34
  600.9 68.7 all-gather.57
  671.8 50.0 all-gather.37
  763.3 84.0 reduce-scatter.36
  863.6 50.4 all-gather.39
  915.5 38.1 all-gather.59
  955.1 39.3 all-gather.61
  996.5 49.9 all-gather.63
  1048.7 84.0 reduce-scatter.38
  1135.5 85.7 reduce-scatter.40
  1240.2 50.4 all-gather.65
  1336.7 84.0 reduce-scatter.42
  1453.5 49.5 all-gather.41
  1519.4 84.0 reduce-scatter.44
  1611.2 50.4 all-gather.67
  1712.6 84.0 reduce-scatter.46
  1799.0 67.0 reduce-scatter.62
  1868.8 66.6 reduce-scatter.60
  1938.2 18.7 reduce-scatter.70
  1959.3 31.5 reduce-scatter.66
  1993.1 18.5 reduce-scatter.68
  2013.9 31.5 reduce-scatter.64
  2048.3 38.0 reduce-scatter.54
  2088.6 38.0 reduce-scatter.58
  2128.8 38.0 reduce-scatter.56
  2169.6 38.0 reduce-scatter.52
  2210.6 53.6 reduce-scatter.48
  2267.0 53.6 reduce-scatter.50
  2324.4 150.8 all-reduce.6
  2476.8 58.5 all-gather.69
  2536.8 57.7 all-gather.71
